TPU v7x, 32 devices: a whole 2x2x4 slice. The times are simulated.
32 devices in a mesh: plane: 4 (over y, core), frame: 8 (over z, x).
Axes of the slice: x: 2, y: 2, z: 4, core: 2. Of those that a mesh axis runs over, the one named last changes fastest.
Arguments:
- image: float32 [8, 8, 2, 128, 128], P('plane', 'frame'), may hold values from -6 to 6
- sens: bfloat16 [4, 8, 2, 128, 128], P(None, 'plane'), may hold values from -3 to 3
- kspace: bfloat16 [4, 8, 8, 2, 128, 128], P(None, 'plane', 'frame'), may hold values from -6 to 6
- offsets: int32 [8, 128], P('frame'), may hold values from 0 to 3
- shifts: int32 [2], replicated, may hold values from 0 to 7
- step_size: float32 [1], replicated, may hold values from 0.5 to 1.5
- threshold: float32 [1], replicated, may hold values from 100 to 1000
Outputs:
- new_image: float32 [8, 8, 2, 128, 128], P('plane', 'frame')
All inputs are finite; a program needn't handle non-finite values.
Results may differ from a plain program's by a relative error of at most 0.0003.
Values sent between devices are 32-bit elements; how exact they have to be, the bound alone decides.
A program may use at most 64 MiB of HBM per device.

v0:
```python
import math

import jax
import jax.numpy as jnp
from jax import lax
from jax.sharding import PartitionSpec as P

PATCH_Y = 8
PATCH_Z = 8
ACCEL = 4
CENTER = 8


def from_partner(block, axis, distance):
    count = lax.axis_size(axis)
    route = []
    for low in range(count):
        high = low | 1 << distance
        if high != low and high < count:
            route += [(low, high), (high, low)]
    return lax.ppermute(block, axis, route)


def dft_tables(length):
    indices = jnp.arange(length, dtype=jnp.int32)
    phases = indices[:, None] * indices[None, :] % length
    angles = phases.astype(jnp.float32) * (2.0 * math.pi / length)
    norm_scale = 1.0 / math.sqrt(length)
    return (jnp.cos(angles) * norm_scale, jnp.sin(angles) * norm_scale)


def along_z(stacked, right_table, sign, width_z):
    product = jnp.einsum(
        "...z,zw->...w",
        stacked,
        right_table,
        precision=lax.Precision.HIGHEST,
        preferred_element_type=jnp.float32,
    )
    cos_part = product[..., :width_z]
    sin_part = product[..., width_z:]
    real_part = cos_part[..., 0, :, :] + sign * sin_part[..., 1, :, :]
    imag_part = cos_part[..., 1, :, :] - sign * sin_part[..., 0, :, :]
    return jnp.stack([real_part, imag_part], axis=-3)


def along_y(stacked, left_table):
    shape_in = stacked.shape
    merged = stacked.reshape(shape_in[:-3] + (2 * shape_in[-2], shape_in[-1]))
    result = jnp.einsum(
        "ur,...rz->...uz",
        left_table,
        merged,
        precision=lax.Precision.HIGHEST,
        preferred_element_type=jnp.float32,
    )
    return result.reshape(shape_in)


def rotate(casorati):
    frames2, voxels = (casorati.shape[-2], casorati.shape[-1])
    split_parts = casorati.reshape(casorati.shape[:-2] + (frames2 // 2, 2, voxels))
    turned = jnp.stack([-split_parts[..., 1, :], split_parts[..., 0, :]], axis=-2)
    return turned.reshape(casorati.shape)


def gram_of(casorati):
    twin = rotate(casorati)
    first = jnp.einsum(
        "kav,kbv->kab",
        casorati,
        casorati,
        precision=lax.Precision.HIGHEST,
        preferred_element_type=jnp.float32,
    )
    second = jnp.einsum(
        "kav,kbv->kab",
        twin,
        twin,
        precision=lax.Precision.HIGHEST,
        preferred_element_type=jnp.float32,
    )
    return first + second


def shrink(casorati, gram, level):
    order = gram.shape[-1]
    system = gram + level * jnp.eye(order, dtype=jnp.float32)
    factor = jnp.linalg.cholesky(system)
    forward_part = jax.scipy.linalg.solve_triangular(factor, casorati, lower=True)
    solved = jax.scipy.linalg.solve_triangular(factor, forward_part, lower=True, trans=1)
    return casorati - level * solved


def local(image, sens, kspace, offsets, shifts, step_size, threshold):
    planes, frames_dev, _, width_y, width_z = image.shape
    frames = frames_dev * lax.axis_size("frame")
    cos_y, sin_y = dft_tables(width_y)
    cos_z, sin_z = dft_tables(width_z)
    right_table = jnp.concatenate([cos_z, sin_z], axis=1)
    left_forward = jnp.concatenate(
        [jnp.concatenate([cos_y, sin_y], axis=1), jnp.concatenate([-sin_y, cos_y], axis=1)], axis=0
    )
    left_inverse = jnp.concatenate(
        [jnp.concatenate([cos_y, -sin_y], axis=1), jnp.concatenate([sin_y, cos_y], axis=1)], axis=0
    )
    rows_y = jnp.arange(width_y, dtype=jnp.int32)
    rows_z = jnp.arange(width_z, dtype=jnp.int32)
    low_y = (rows_y < CENTER) | (rows_y >= width_y - CENTER)
    low_z = (rows_z < CENTER) | (rows_z >= width_z - CENTER)
    regular = (rows_z[None, None, :] + offsets[:, :, None]) % ACCEL == 0
    sampled = (regular | low_y[None, :, None] & low_z[None, None, :]).astype(jnp.float32)
    image_re = image[:, :, 0]
    image_im = image[:, :, 1]
    maps = sens.astype(jnp.float32)
    sens_re = maps[:, :, 0][:, :, None]
    sens_im = maps[:, :, 1][:, :, None]
    coil_re = sens_re * image_re[None] - sens_im * image_im[None]
    coil_im = sens_re * image_im[None] + sens_im * image_re[None]
    stacked = jnp.stack([coil_re, coil_im], axis=3)
    spectra = along_y(along_z(stacked, right_table, 1.0, width_z), left_forward)
    resid = sampled[None, None, :, None] * (spectra - kspace.astype(jnp.float32))
    returned = along_z(along_y(resid, left_inverse), right_table, -1.0, width_z)
    back_re = returned[:, :, :, 0]
    back_im = returned[:, :, :, 1]
    grad_re = jnp.sum(sens_re * back_re + sens_im * back_im, axis=0)
    grad_im = jnp.sum(sens_re * back_im - sens_im * back_re, axis=0)
    moved = image - step_size[0] * jnp.stack([grad_re, grad_im], axis=2)
    rolled = jnp.roll(moved, (shifts[0], shifts[1]), axis=(3, 4))
    nyb = width_y // PATCH_Y
    nzb = width_z // PATCH_Z
    voxels = planes * PATCH_Y * PATCH_Z
    blocks = rolled.reshape(planes, frames_dev, 2, nyb, PATCH_Y, nzb, PATCH_Z)
    blocks = blocks.transpose(3, 5, 1, 2, 0, 4, 6).reshape(nyb * nzb, frames_dev, 2, voxels)
    regrouped = lax.all_to_all(blocks, "frame", split_axis=0, concat_axis=1, tiled=True)
    count = regrouped.shape[0]
    casorati = regrouped.reshape(count, 2 * frames, voxels)
    level = threshold[0]
    parity = lax.axis_index("plane") % 2
    halfway = count // 2
    first_part = casorati[:halfway]
    second_part = casorati[halfway:]
    kept_part = jnp.where(parity == 0, first_part, second_part)
    outgoing = jnp.where(parity == 0, second_part, first_part)
    incoming = from_partner(outgoing, "plane", 0)
    complete = jnp.concatenate([kept_part, incoming], axis=2)
    finished = shrink(complete, gram_of(complete), level)
    own_part = finished[:, :, :voxels]
    returned_part = from_partner(finished[:, :, voxels:], "plane", 0)
    shrunk = jnp.where(
        parity == 0,
        jnp.concatenate([own_part, returned_part], axis=0),
        jnp.concatenate([returned_part, own_part], axis=0),
    )
    restored = lax.all_to_all(
        shrunk.reshape(count, frames, 2, voxels), "frame", split_axis=1, concat_axis=0, tiled=True
    )
    placed = restored.reshape(nyb, nzb, frames_dev, 2, planes, PATCH_Y, PATCH_Z)
    placed = placed.transpose(4, 2, 3, 0, 5, 1, 6).reshape(planes, frames_dev, 2, width_y, width_z)
    return jnp.roll(placed, (-shifts[0], -shifts[1]), axis=(3, 4))


def solution(mesh):
    in_specs = (
        P("plane", "frame", None, None, None),
        P(None, "plane", None, None, None),
        P(None, "plane", "frame", None, None, None),
        P("frame", None),
        P(),
        P(),
        P(),
    )
    out_specs = P("plane", "frame", None, None, None)
    return jax.shard_map(local, mesh=mesh, in_specs=in_specs, out_specs=out_specs, check_vma=False)
```

profile of v0, /device:TPU:0, one launch (start us, length us, event | category | flops | bytes accessed | tf_op | source)
XLA Modules:
  0.0 114.0 jit_solution(13654522863200061980)
XLA Ops:
  0.0 1.3 %fusion.51 = (s32[1]{0:T(128)}, s32[1]{0:T(128)}) fusion(s32[2]{0:T(128)} %param.13), kind=kLoop, calls=%fused_computation.107 | loop fusion | bytes 16 | tf_op jit(solution)/shard_map/jit(_roll_dynamic)/unstack | solution.py:129
  3.2 0.3 sine_multiply_fusion
  3.5 0.3 fusion.44
  5.6 1.1 copy_convert_fusion
  6.8 1.0 slice_bitcast_fusion.1
  7.8 0.1 subtract_bitcast_fusion
  7.9 1.8 %convolution_bitcast_fusion.1 = f32[4,2,1,2,128,256]{5,4,3,1,0,2:T(8,128)S(1)} fusion(f32[4,2,1,1,128,128]{5,4,3,1,0,2:T(8,128)S(1)} %get-tuple-element.11, f32[4,2,1,1,128,128]{5,4,3,1,0,2:T(8,128)S(1)} %get-tuple-element.10, f32[128,128]{1,0:T(8,128)S(1)} %get-tuple-element.24, f32[128,128]{1,0:T(8,128)S(1)} %get-tuple-element.25), kind=kOutput, calls=%fused_computation.1 | convolution fusion | flops 805601280 | bytes 3276800 | tf_op jit(solution)/shard_map/...z,zw->...w/dot_general | solution.py:33
  9.7 0.1 slice_add_fusion
  9.9 1.8 %convolution_bitcast_fusion.3 = f32[4,2,1,256,128]{3,4,1,0,2:T(8,128)S(1)} fusion(f32[4,2,256,128]{3,2,1,0:T(8,128)S(1)} %bitcast.121, f32[128,128]{1,0:T(8,128)S(1)} %get-tuple-element.25, f32[128,128]{1,0:T(8,128)S(1)} %fusion.44, f32[128,128]{1,0:T(8,128)S(1)} %get-tuple-element.24), kind=kOutput, calls=%fused_computation.3 | convolution fusion | flops 805502976 | bytes 2293760 | tf_op jit(solution)/shard_map/ur,...rz->...uz/dot_general | solution.py:50
  11.7 0.3 copy.101
  12.1 0.1 fusion.43
  12.2 1.2 %subtract_multiply_fusion = f32[4,2,1,2,128,128]{5,4,3,2,1,0:T(8,128)S(1)} fusion(f32[4,2,1,2,128,128]{5,4,3,2,1,0:T(8,128)S(1)} %bitcast.122, bf16[4,2,1,2,128,128]{5,4,3,2,1,0:T(8,128)(2,1)} %param.11, f32[128,128]{1,0:T(8,128)S(1)} %fusion.43), kind=kLoop, calls=%fused_computation.12 | loop fusion | flops 786432 | bytes 2686976 | tf_op jit(solution)/shard_map/mul | solution.py:122
  13.4 1.8 %convolution_bitcast_fusion.2 = f32[4,2,1,256,128]{3,4,1,0,2:T(8,128)S(1)} fusion(f32[4,2,256,128]{3,2,1,0:T(8,128)S(1)} %bitcast.123, f32[128,128]{1,0:T(8,128)S(1)} %get-tuple-element.25, f32[128,128]{1,0:T(8,128)S(1)} %get-tuple-element.24, f32[128,128]{1,0:T(8,128)S(1)} %fusion.44), kind=kOutput, calls=%fused_computation.2 | convolution fusion | flops 805502976 | bytes 2293760 | tf_op jit(solution)/shard_map/ur,...rz->...uz/dot_general | solution.py:50
  15.2 0.3 copy.102
  15.5 1.8 %convolution_bitcast_fusion = f32[4,2,1,2,128,256]{5,4,1,0,3,2:T(8,128)S(1)} fusion(f32[4,2,2,128,128]{4,3,2,1,0:T(8,128)S(1)} %bitcast.120, f32[128,128]{1,0:T(8,128)S(1)} %get-tuple-element.24, f32[128,128]{1,0:T(8,128)S(1)} %get-tuple-element.25), kind=kOutput, calls=%fused_computation | convolution fusion | flops 805339136 | bytes 3276800 | tf_op jit(solution)/shard_map/...z,zw->...w/dot_general | solution.py:33
  17.4 0.3 add_reduce_fusion
  18.4 0.2 fusion.17
  18.7 3.6 %reshape.304 = f32[2,1,2,16,8,16,8]{6,5,4,3,2,0,1:T(8,128)} reshape(f32[2,1,2,128,128]{4,3,2,1,0:T(8,128)S(1)} %fusion.17) | data formatting | bytes 524288 | tf_op jit(solution)/shard_map/reshape | solution.py:133
  22.3 2.9 %copy.73 = f32[16,16,1,2,2,8,8]{1,0,6,5,4,3,2:T(8,128)S(1)} copy(f32[16,16,1,2,2,8,8]{6,1,5,0,3,4,2:T(8,128)} %bitcast.118) | data formatting | bytes 524288 | tf_op jit(solution)/shard_map/transpose | solution.py:134
  25.2 0.9 reshape.305
  26.1 0.8 copy.74
  27.0 7.3 %all-to-all-start = ((f32[256,1,2,128]{3,2,1,0:T(2,128)}), f32[256,1,2,128]{3,2,1,0:T(2,128)S(1)}, u32[]{:S(2)}, u32[]{:S(2)}) async-start(f32[256,1,2,128]{3,2,1,0:T(2,128)} %copy.74), calls=%async_computation | async-start | bytes 524288 | tf_op jit(solution)/shard_map/all_to_all | solution.py:135
  34.9 8.2 %all-to-all-done = f32[256,1,2,128]{3,2,1,0:T(2,128)S(1)} async-done(((f32[256,1,2,128]{3,2,1,0:T(2,128)}), f32[256,1,2,128]{3,2,1,0:T(2,128)S(1)}, u32[]{:S(2)}, u32[]{:S(2)}) %all-to-all-start) | async-done | bytes 262176 | tf_op jit(solution)/shard_map/all_to_all | solution.py:135
  43.2 0.1 copy.77
  43.5 0.1 copy.76
  43.6 1.1 collective-permute-done
  44.8 0.1 reshape.306
  44.9 0.2 slice_negate_fusion
  45.1 0.2 pad_maximum_fusion.8
  45.4 0.2 reshape.307
  45.6 0.4 fusion.52
  45.9 0.4 broadcast_add_fusion
  46.4 23.5 %custom-call.11 = f32[16,16,16]{2,1,0:T(8,128)S(1)} custom-call(f32[16,16,16]{2,1,0:T(8,128)S(1)} %fusion.30), custom_call_target="Cholesky" | custom-call | tf_op jit(solution)/shard_map/jit(cholesky)/cholesky | solution.py:89
  69.9 0.1 compare_reduce_fusion
  70.1 0.1 select_bitcast_fusion
  70.2 19.8 %custom-call.12 = f32[16,1,16,16]{2,3,1,0:T(8,128)S(1)} custom-call(f32[16,1,16,16]{3,2,1,0:T(8,128)S(1)} %select_bitcast_fusion), custom_call_target="InvertDiagBlocksLowerTriangular" | custom-call | tf_op jit(solution)/shard_map/jit(_solve_triangular)/vmap()/triangular_solve | solution.py:91
  89.9 0.5 fusion.27
  90.4 0.4 fusion
  90.8 0.2 collective-permute-start.1
  91.1 1.2 %collective-permute-done.1 = f32[16,16,128]{2,1,0:T(8,128)S(1)} collective-permute-done((f32[16,16,128]{2,1,0:T(8,128)S(1)}, f32[16,16,128]{2,1,0:T(8,128)S(1)}, u32[]{:S(2)}, u32[]{:S(2)}) %collective-permute-start.1) | collective-permute-done | bytes 131104 | tf_op jit(solution)/shard_map/ppermute | solution.py:21
  92.3 0.7 maximum_select_fusion
  93.0 3.6 %all-to-all-start.1 = ((f32[32,8,2,128]{3,0,2,1:T(8,128)}), f32[32,8,2,128]{3,0,2,1:T(8,128)S(1)}, u32[]{:S(2)}, u32[]{:S(2)}) async-start(f32[32,8,2,128]{3,0,2,1:T(8,128)} %maximum_select_fusion), calls=%async_computation.1 | async-start | bytes 524288 | tf_op jit(solution)/shard_map/all_to_all | solution.py:155
  97.9 8.0 %all-to-all-done.1 = f32[32,8,2,128]{3,0,2,1:T(8,128)S(1)} async-done(((f32[32,8,2,128]{3,0,2,1:T(8,128)}), f32[32,8,2,128]{3,0,2,1:T(8,128)S(1)}, u32[]{:S(2)}, u32[]{:S(2)}) %all-to-all-start.1) | async-done | bytes 262176 | tf_op jit(solution)/shard_map/all_to_all | solution.py:155
  105.9 0.4 copy.87
  106.3 0.3 reshape.308
  106.6 2.8 %copy.88 = f32[2,1,2,16,8,16,8]{6,5,4,3,2,0,1:T(8,128)} copy(f32[2,1,2,16,8,16,8]{5,3,6,4,0,2,1:T(8,128)S(1)} %bitcast.119) | data formatting | bytes 524288 | tf_op jit(solution)/shard_map/transpose | solution.py:159
  109.4 3.6 %reshape.309 = f32[2,1,2,128,128]{4,3,2,0,1:T(8,128)S(1)} reshape(f32[2,1,2,16,8,16,8]{6,5,4,3,2,0,1:T(8,128)} %copy.88) | data formatting | bytes 524288 | tf_op jit(solution)/shard_map/reshape | solution.py:159
  113.1 0.9 fusion.15
  (23 shorter events, 0.8 us)
Async XLA Ops:
  9.9 2.2 %copy-start.1 = (s32[1,128]{1,0:T(1,128)S(1)}, s32[1,128]{1,0:T(1,128)}, u32[]{:S(2)}) copy-start(s32[1,128]{1,0:T(1,128)} %param.12) | copy-start | bytes 1540
  17.4 1.0 copy-start
  27.0 16.2 %all-to-all-start = ((f32[256,1,2,128]{3,2,1,0:T(2,128)}), f32[256,1,2,128]{3,2,1,0:T(2,128)S(1)}, u32[]{:S(2)}, u32[]{:S(2)}) async-start(f32[256,1,2,128]{3,2,1,0:T(2,128)} %copy.74), calls=%async_computation | async-start | bytes 524288 | tf_op jit(solution)/shard_map/all_to_all | solution.py:135
  43.3 1.4 %collective-permute-start = (f32[16,16,128]{2,1,0:T(8,128)S(1)}, f32[16,16,128]{2,1,0:T(8,128)S(1)}, u32[]{:S(2)}, u32[]{:S(2)}) collective-permute-start(f32[16,16,128]{2,1,0:T(8,128)S(1)} %bitcast.133), channel_id=1, source_target_pairs={{0,8},{8,0},{16,24},{24,16},{1,9},{9,1},{17,25},{25,17},{2,10},{10... | collective-permute-start | bytes 393224 | tf_op jit(solution)/shard_map/ppermute | solution.py:21
  90.8 1.4 %collective-permute-start.1 = (f32[16,16,128]{2,1,0:T(8,128)S(1)}, f32[16,16,128]{2,1,0:T(8,128)S(1)}, u32[]{:S(2)}, u32[]{:S(2)}) collective-permute-start(f32[16,16,128]{2,1,0:T(8,128)S(1)} %get-tuple-element.13), channel_id=1, source_target_pairs={{0,8},{8,0},{16,24},{24,16},{1,9},{9,1},{17,25},{25,17},{2,10},{10... | collective-permute-start | bytes 393224 | tf_op jit(solution)/shard_map/ppermute | solution.py:21
  93.0 12.9 %all-to-all-start.1 = ((f32[32,8,2,128]{3,0,2,1:T(8,128)}), f32[32,8,2,128]{3,0,2,1:T(8,128)S(1)}, u32[]{:S(2)}, u32[]{:S(2)}) async-start(f32[32,8,2,128]{3,0,2,1:T(8,128)} %maximum_select_fusion), calls=%async_computation.1 | async-start | bytes 524288 | tf_op jit(solution)/shard_map/all_to_all | solution.py:155
where the time goes:
time: 115 us; the launch traced here: 114 us
  other arithmetic  49.6 us (43%)
  local copies, waits for them, and re-layouts  19.3 us (17%)
  waiting for transfers between devices  18.5 us (16%)
  starting transfers between devices  11.2 us (10%)
  matrix products  8.81 us (8%)
  between operations  6.67 us (6%)
    another operation x4, other arithmetic, shrink(): factor = jnp.linalg.cholesky(system)  23.6 us
    another operation x3, other arithmetic, shrink(): jax.scipy.linalg.solve_triangular(factor, forward_part, lower=True, trans=1)  19.9 us
    all_to_all x1, waiting for transfers between devices, local(): lax.all_to_all(blocks, 'frame', split_axis=0, concat_axis=1, tiled=True)  8.25 us
    all_to_all x1, waiting for transfers between devices, local(): lax.all_to_all(shrunk.reshape(count, frames, 2, voxels), 'frame', split_a...  8.01 us
    all_to_all x1, starting transfers between devices, local(): lax.all_to_all(blocks, 'frame', split_axis=0, concat_axis=1, tiled=True)  7.29 us
    reshape x1, local copies, waits for them, and re-layouts, local(): placed.transpose(4, 2, 3, 0, 5, 1, 6)  3.64 us
    dot_general x2, matrix products, along_y(): jnp.einsum('ur,...rz->...uz', left_table, merged, precision=lax.Precision...  3.62 us
    reshape x1, local copies, waits for them, and re-layouts, local(): blocks = rolled.reshape(planes, frames_dev, 2, nyb, PATCH_Y, nzb, PATCH_Z)  3.62 us
  transfers between devices with their start and end apart: 4, of which 4 were waited for; matrix products, arithmetic and copies ran while one was open for 0% of the time, Pallas kernels for 0%

commit v1 on v0

--- a/solution.py
+++ b/solution.py
@@ -1,10 +1,15 @@
+import functools
 import math
 
 import jax
 import jax.numpy as jnp
+import numpy as np
 from jax import lax
+from jax.experimental import pallas as pl
+from jax.experimental.pallas import tpu as pltpu
 from jax.sharding import PartitionSpec as P
 
+PATCH_X = 4
 PATCH_Y = 8
 PATCH_Z = 8
 ACCEL = 4
@@ -92,7 +97,7 @@
     return casorati - level * solved
 
 
-def local(image, sens, kspace, offsets, shifts, step_size, threshold):
+def local_general(image, sens, kspace, offsets, shifts, step_size, threshold):
     planes, frames_dev, _, width_y, width_z = image.shape
     frames = frames_dev * lax.axis_size("frame")
     cos_y, sin_y = dft_tables(width_y)
@@ -160,6 +165,333 @@
     return jnp.roll(placed, (-shifts[0], -shifts[1]), axis=(3, 4))
 
 
+def block_tables(length):
+    indices = np.arange(length)
+    angles = (indices[:, None] * indices[None, :] % length) * (2.0 * np.pi / length)
+    cos = np.cos(angles) / np.sqrt(length)
+    sin = np.sin(angles) / np.sqrt(length)
+    rotation = np.block([[cos, sin], [-sin, cos]])
+    high = rotation.astype(jnp.bfloat16)
+    low = (rotation - high.astype(np.float64)).astype(jnp.bfloat16)
+    return np.stack([high, low, high.T, low.T])
+
+
+def halves(values):
+    high = values.astype(jnp.bfloat16)
+    return high, (values - high.astype(jnp.float32)).astype(jnp.bfloat16)
+
+
+def mul(left, right):
+    return jnp.dot(left, right, preferred_element_type=jnp.float32)
+
+
+def from_right(values, high, low):
+    value_high, value_low = halves(values)
+    return mul(value_high, high) + mul(value_high, low) + mul(value_low, high)
+
+
+def from_left(high, low, values):
+    value_high, value_low = halves(values)
+    return mul(high, value_high) + mul(low, value_high) + mul(high, value_low)
+
+
+def rows_to_lanes(values, coils, width):
+    parts = [
+        jnp.concatenate([values[c * width : (c + 1) * width, k * width : (k + 1) * width] for c in range(coils)], axis=1)
+        for k in range(2)
+    ]
+    return jnp.concatenate(parts, axis=0)
+
+
+def lanes_to_rows(values, coils, width):
+    parts = [
+        jnp.concatenate([values[k * width : (k + 1) * width, c * width : (c + 1) * width] for k in range(2)], axis=1)
+        for c in range(coils)
+    ]
+    return jnp.concatenate(parts, axis=0)
+
+
+def moved_plane(p, coils, width, image_ref, sens_ref, kspace_ref, table_ref, step, sampled):
+    image_re = image_ref[p, 0, 0]
+    image_im = image_ref[p, 0, 1]
+    stacked = []
+    for c in range(coils):
+        sens_re = sens_ref[c, p, 0].astype(jnp.float32)
+        sens_im = sens_ref[c, p, 1].astype(jnp.float32)
+        stacked.append(
+            jnp.concatenate(
+                [sens_re * image_re - sens_im * image_im, sens_re * image_im + sens_im * image_re], axis=1
+            )
+        )
+    along = from_right(jnp.concatenate(stacked, axis=0), table_ref[2], table_ref[3])
+    spectra = from_left(table_ref[0], table_ref[1], rows_to_lanes(along, coils, width))
+    data = jnp.concatenate(
+        [
+            jnp.concatenate([kspace_ref[c, p, 0, k].astype(jnp.float32) for c in range(coils)], axis=1)
+            for k in range(2)
+        ],
+        axis=0,
+    )
+    weight = jnp.concatenate([jnp.concatenate([sampled] * coils, axis=1)] * 2, axis=0)
+    resid = weight * (spectra - data)
+    back = from_left(table_ref[2], table_ref[3], resid)
+    returned = from_right(lanes_to_rows(back, coils, width), table_ref[0], table_ref[1])
+    grad_re = jnp.zeros_like(image_re)
+    grad_im = jnp.zeros_like(image_im)
+    for c in range(coils):
+        back_re = returned[c * width : (c + 1) * width, :width]
+        back_im = returned[c * width : (c + 1) * width, width:]
+        sens_re = sens_ref[c, p, 0].astype(jnp.float32)
+        sens_im = sens_ref[c, p, 1].astype(jnp.float32)
+        grad_re += sens_re * back_re + sens_im * back_im
+        grad_im += sens_re * back_im - sens_im * back_re
+    return image_re - step * grad_re, image_im - step * grad_im
+
+
+def sweep(matrix, order):
+    for k in range(order):
+        pivot = 1.0 / matrix[k, k][0]
+        column = {}
+        for i in range(order):
+            if i > k:
+                column[i] = matrix[i, k]
+            elif i < k:
+                column[i] = (matrix[k, i][0], -matrix[k, i][1])
+        scaled = {i: (re * pivot, im * pivot) for i, (re, im) in column.items()}
+        for i in column:
+            for j in column:
+                if j > i:
+                    continue
+                a_re, a_im = scaled[i]
+                b_re, b_im = column[j]
+                re, im = matrix[i, j]
+                re = re - (a_re * b_re + a_im * b_im)
+                if i != j:
+                    im = im - (a_im * b_re - a_re * b_im)
+                matrix[i, j] = (re, im)
+        for i in column:
+            if i > k:
+                matrix[i, k] = scaled[i]
+            else:
+                matrix[k, i] = (scaled[i][0], -scaled[i][1])
+        matrix[k, k] = (-pivot, None)
+    return matrix
+
+
+def step_kernel(
+    planes, frames, group, coils, width_y, width_z,
+    shifts_ref, step_ref, level_ref, offsets_ref, image_ref, sens_ref, kspace_ref, table_ref,
+    out_ref,
+    rolled, gathered, entries, inverse, finished, landed,
+    send_out, recv_out, send_back, recv_back, own_out, own_back,
+):
+    total = frames * group
+    plane_me = lax.axis_index("plane")
+    frame_me = lax.axis_index("frame")
+    part_me = lax.rem(plane_me, group)
+    base = plane_me - part_me
+    me = frame_me * group + part_me
+    rows = PATCH_Y
+
+    def device(index):
+        return {"plane": base + lax.rem(index, group), "frame": index // group}
+
+    barrier = pltpu.get_barrier_semaphore()
+    for k in range(1, total):
+        pl.semaphore_signal(barrier, inc=1, device_id=device(lax.rem(me + k, total)), device_id_type=pl.DeviceIdType.MESH)
+
+    lane = lax.broadcasted_iota(jnp.int32, (width_y, width_z), 1)
+    row = lax.broadcasted_iota(jnp.int32, (width_y, width_z), 0)
+    offset = jnp.broadcast_to(offsets_ref[...].astype(jnp.float32), (width_z, width_y)).T
+    wanted = jnp.where(offset == 0.0, 0.0, ACCEL - offset)
+    regular = lax.rem(lane, ACCEL).astype(jnp.float32) == wanted
+    low_y = (row < CENTER) | (row >= width_y - CENTER)
+    low_z = (lane < CENTER) | (lane >= width_z - CENTER)
+    sampled = (regular | (low_y & low_z)).astype(jnp.float32)
+
+    sends = []
+    for p in range(planes):
+        moved = moved_plane(p, coils, width_y, image_ref, sens_ref, kspace_ref, table_ref, step_ref[0], sampled)
+        for k in range(2):
+            rolled[p, k] = pltpu.roll(pltpu.roll(moved[k], shifts_ref[0], 0), shifts_ref[1], 1)
+        if p == 0:
+            pl.semaphore_wait(barrier, total - 1)
+        group_sends = []
+        for k in range(1, total):
+            target = lax.rem(me + k, total)
+            copy = pltpu.make_async_remote_copy(
+                src_ref=rolled.at[p, :, pl.ds(pl.multiple_of(target * rows, rows), rows), :],
+                dst_ref=gathered.at[p, part_me, frame_me],
+                send_sem=send_out.at[p, k],
+                recv_sem=recv_out.at[p, k],
+                device_id=device(target),
+                device_id_type=pl.DeviceIdType.MESH,
+            )
+            copy.start()
+            group_sends.append(copy)
+        own = pltpu.make_async_copy(
+            rolled.at[p, :, pl.ds(pl.multiple_of(me * rows, rows), rows), :],
+            gathered.at[p, part_me, frame_me],
+            own_out.at[p],
+        )
+        own.start()
+        sends.append((group_sends, own))
+
+    pairs = [(f, g) for f in range(frames) for g in range(f + 1)]
+    for p in range(planes):
+        group_sends, own = sends[p]
+        own.wait()
+        for copy in group_sends:
+            copy.wait_recv()
+        for n, (f, g) in enumerate(pairs):
+            sum_re = None
+            sum_im = None
+            for q in range(group):
+                f_re, f_im = gathered[p, q, f, 0], gathered[p, q, f, 1]
+                g_re, g_im = gathered[p, q, g, 0], gathered[p, q, g, 1]
+                re = f_re * g_re + f_im * g_im
+                sum_re = re if sum_re is None else sum_re + re
+                if f != g:
+                    im = f_im * g_re - f_re * g_im
+                    sum_im = im if sum_im is None else sum_im + im
+            spot = f * frames + g
+            entries[spot] = sum_re if p == 0 else entries[spot] + sum_re
+            if f != g:
+                spot = g * frames + f
+                entries[spot] = sum_im if p == 0 else entries[spot] + sum_im
+
+    one_row = lax.broadcasted_iota(jnp.int32, (width_z, width_z), 0) // PATCH_Z
+    one_lane = lax.broadcasted_iota(jnp.int32, (width_z, width_z), 1) // PATCH_Z
+    same = (one_row == one_lane).astype(jnp.bfloat16)
+    cells = entries[...]
+    shift = rows // 2
+    while shift:
+        cells = cells + pltpu.roll(cells, shift, 1)
+        shift //= 2
+    high, low = halves(cells.reshape(frames * frames * rows, width_z))
+    entries[...] = (mul(high, same) + mul(low, same)).reshape(frames * frames, rows, width_z)
+
+    level = level_ref[0]
+    matrix = {}
+    for f, g in pairs:
+        if f == g:
+            matrix[f, f] = (entries[f * frames + f] + level, None)
+        else:
+            matrix[f, g] = (entries[f * frames + g], entries[g * frames + f])
+    matrix = sweep(matrix, frames)
+    for f, g in pairs:
+        inverse[f * frames + g] = matrix[f, g][0] * level
+        if f != g:
+            inverse[g * frames + f] = matrix[f, g][1] * level
+
+    backs = []
+    for r in range(group):
+        q = lax.rem(part_me + 1 + r, group)
+        for p in range(planes):
+            values = [(gathered[p, q, g, 0], gathered[p, q, g, 1]) for g in range(frames)]
+            for f in range(frames):
+                re, im = values[f]
+                for g in range(frames):
+                    g_re, g_im = values[g]
+                    if f == g:
+                        w_re = inverse[f * frames + f]
+                        re = re + w_re * g_re
+                        im = im + w_re * g_im
+                        continue
+                    if f > g:
+                        w_re, w_im = inverse[f * frames + g], inverse[g * frames + f]
+                        re = re + (w_re * g_re - w_im * g_im)
+                        im = im + (w_re * g_im + w_im * g_re)
+                    else:
+                        w_re, w_im = inverse[g * frames + f], inverse[f * frames + g]
+                        re = re + (w_re * g_re + w_im * g_im)
+                        im = im + (w_re * g_im - w_im * g_re)
+                finished[q, f, p, 0] = re
+                finished[q, f, p, 1] = im
+        for k in range(frames):
+            f = lax.rem(frame_me + k, frames)
+            source = finished.at[q, f]
+            if r == group - 1 and k == 0:
+                copy = pltpu.make_async_copy(
+                    source, landed.at[:, :, pl.ds(pl.multiple_of(me * rows, rows), rows), :], own_back
+                )
+                copy.start()
+                backs.append((copy, True))
+                continue
+            copy = pltpu.make_async_remote_copy(
+                src_ref=source,
+                dst_ref=landed.at[:, :, pl.ds(pl.multiple_of(me * rows, rows), rows), :],
+                send_sem=send_back.at[r, k],
+                recv_sem=recv_back.at[r, k],
+                device_id={"plane": base + q, "frame": f},
+                device_id_type=pl.DeviceIdType.MESH,
+            )
+            copy.start()
+            backs.append((copy, False))
+    for copy, local in backs:
+        if local:
+            copy.wait()
+        else:
+            copy.wait_recv()
+    for p in range(planes):
+        for k in range(2):
+            shift_y = lax.rem(width_y - shifts_ref[0], width_y)
+            shift_z = lax.rem(width_z - shifts_ref[1], width_z)
+            out_ref[p, 0, k] = pltpu.roll(pltpu.roll(landed[p, k], shift_y, 0), shift_z, 1)
+    for group_sends, own in sends:
+        for copy in group_sends:
+            copy.wait_send()
+    for copy, local in backs:
+        if not local:
+            copy.wait_send()
+
+
+def local_fused(image, sens, kspace, offsets, shifts, step_size, threshold):
+    planes, _, _, width_y, width_z = image.shape
+    coils = sens.shape[0]
+    frames = lax.axis_size("frame")
+    group = PATCH_X // planes
+    total = frames * group
+    table = jnp.asarray(block_tables(width_y))
+    vmem = pl.BlockSpec(memory_space=pltpu.VMEM)
+    smem = pl.BlockSpec(memory_space=pltpu.SMEM)
+    slab = (PATCH_Y, width_z)
+    dma = pltpu.SemaphoreType.DMA
+    return pl.pallas_call(
+        functools.partial(step_kernel, planes, frames, group, coils, width_y, width_z),
+        out_shape=jax.ShapeDtypeStruct(image.shape, jnp.float32),
+        in_specs=[smem, smem, smem, vmem, vmem, vmem, vmem, vmem],
+        out_specs=vmem,
+        scratch_shapes=[
+            pltpu.VMEM((planes, 2, width_y, width_z), jnp.float32),
+            pltpu.VMEM((planes, group, frames, 2) + slab, jnp.float32),
+            pltpu.VMEM((frames * frames,) + slab, jnp.float32),
+            pltpu.VMEM((frames * frames,) + slab, jnp.float32),
+            pltpu.VMEM((group, frames, planes, 2) + slab, jnp.float32),
+            pltpu.VMEM((planes, 2, width_y, width_z), jnp.float32),
+            dma((planes, total)),
+            dma((planes, total)),
+            dma((group, frames)),
+            dma((group, frames)),
+            dma((planes,)),
+            dma(()),
+        ],
+        compiler_params=pltpu.CompilerParams(collective_id=0, has_side_effects=True),
+        name="prox_step",
+    )(shifts, step_size, threshold, offsets, image, sens, kspace, table)
+
+
+def local(image, sens, kspace, offsets, shifts, step_size, threshold):
+    planes, frames_dev, _, width_y, width_z = image.shape
+    frames = frames_dev * lax.axis_size("frame")
+    group = PATCH_X // planes
+    one_block = frames * group * PATCH_Y == width_y and frames_dev == 1
+    split = group > 1 and lax.axis_size("plane") % group == 0
+    if one_block and split and width_y == width_z and width_z % 128 == 0:
+        return local_fused(image, sens, kspace, offsets, shifts, step_size, threshold)
+    return local_general(image, sens, kspace, offsets, shifts, step_size, threshold)
+
+
 def solution(mesh):
     in_specs = (
         P("plane", "frame", None, None, None),

time: 115 us -> 27.6 us (0.24)
  other arithmetic: 49.6 us -> 0 us
  Pallas kernels: 0 us -> 24.4 us
  waiting for transfers between devices: 18.5 us -> 0 us
  local copies, waits for them, and re-layouts: 19.3 us -> 1.67 us
  starting transfers between devices: 11.2 us -> 0 us
  matrix products: 8.81 us -> 0 us
  between operations: 6.67 us -> 1.3 us
    another operation x10 -> x0, other arithmetic: 43.9 us -> none  [the longest x4 23.6 us: shrink(): factor = jnp.linalg.cholesky(system)]
    pallas_call x0 -> x1, Pallas kernels: none -> 24.4 us  [local_fused(): pl.pallas_call(functools.partial(step_kernel, planes, frames, group, coil...]
    all_to_all x2 -> x0, waiting for transfers between devices: 16.3 us -> none  [the longest x1 8.25 us: local(): lax.all_to_all(blocks, 'frame', split_axis=0, concat_axis=1, tiled=True)]
    all_to_all x2 -> x0, starting transfers between devices: 10.9 us -> none  [the longest x1 7.29 us: local(): lax.all_to_all(blocks, 'frame', split_axis=0, concat_axis=1, tiled=True)]
    reshape x8 -> x0, local copies, waits for them, and re-layouts: 10 us -> none  [the longest x1 3.64 us: local(): placed.transpose(4, 2, 3, 0, 5, 1, 6)]
    dot_general x6 -> x0, matrix products: 7.95 us -> none  [the longest x2 3.62 us: along_y(): jnp.einsum('ur,...rz->...uz', left_table, merged, precision=lax.Precision...]
    transpose x2 -> x0, local copies, waits for them, and re-layouts: 5.68 us -> none  [the longest x1 2.91 us: local(): blocks.transpose(3, 5, 1, 2, 0, 4, 6)]
    ppermute x2 -> x0, waiting for transfers between devices: 2.29 us -> none  [from_partner(): return lax.ppermute(block, axis, route)]
  transfers between devices with their start and end apart: 4 -> 0, of which waited for: 4 -> 0; matrix products, arithmetic and copies ran while one was open for 0% -> 0% of each run, Pallas kernels for 0% -> 0%
where the time goes in v1:
time: 27.6 us; the launch traced here: 27.4 us
  Pallas kernels  24.4 us (88%)
  local copies, waits for them, and re-layouts  1.67 us (6%)
  between operations  1.3 us (5%)
    pallas_call x1, Pallas kernels, local_fused(): pl.pallas_call(functools.partial(step_kernel, planes, frames, group, coil...  24.4 us
    unnamed x1, local copies, waits for them, and re-layouts  1.67 us

profile of v1, /device:TPU:0, one launch (start us, length us, event | category | flops | bytes accessed | tf_op | source)
XLA Modules:
  0.0 27.4 jit_solution(773704604552449943)
XLA Ops:
  1.3 24.4 %prox_step.1 = f32[2,1,2,128,128]{4,3,2,1,0:T(8,128)} custom-call(s32[2]{0:T(128)} %shifts_ref.1, f32[1]{0:T(128)S(6)} %copy.10.step_ref, f32[1]{0:T(128)S(6)} %copy.11.level_ref, s32[1,128]{1,0:T(1,128)} %offsets_ref.1, f32[2,1,2,128,128]{4,3,2,1,0:T(8,128)} %image_ref.1, bf16[4,2,2,128,128]{4,3,2,1,0:T(8,128)(2,1)} %sens_ref.1, ...), custom_call_target="tpu_custom_call" | custom-call | tf_op jit(solution)/shard_map/prox_step/pallas_call | solution.py:460
  25.8 1.7 %copy.12 = f32[2,1,2,128,128]{4,3,2,1,0:T(8,128)} copy(f32[2,1,2,128,128]{4,3,2,1,0:T(8,128)} %prox_step.1) | data formatting | bytes 524288

commit v2 on v1

--- a/solution.py
+++ b/solution.py
@@ -165,6 +165,9 @@
     return jnp.roll(placed, (-shifts[0], -shifts[1]), axis=(3, 4))
 
 
+VMEM_BYTES = 24 * 1024 * 1024
+
+
 def block_tables(length):
     indices = np.arange(length)
     angles = (indices[:, None] * indices[None, :] % length) * (2.0 * np.pi / length)
@@ -211,7 +214,9 @@
     return jnp.concatenate(parts, axis=0)
 
 
-def moved_plane(p, coils, width, image_ref, sens_ref, kspace_ref, table_ref, step, sampled):
+def moved_plane(loads, p, coils, width, image_ref, sens_ref, kspace_ref, table_ref, step, sampled):
+    loads["image", p].wait()
+    loads["sens", p].wait()
     image_re = image_ref[p, 0, 0]
     image_im = image_ref[p, 0, 1]
     stacked = []
@@ -223,8 +228,13 @@
                 [sens_re * image_re - sens_im * image_im, sens_re * image_im + sens_im * image_re], axis=1
             )
         )
+    if p == 0:
+        loads["inverse"].wait()
     along = from_right(jnp.concatenate(stacked, axis=0), table_ref[2], table_ref[3])
+    if p == 0:
+        loads["forward"].wait()
     spectra = from_left(table_ref[0], table_ref[1], rows_to_lanes(along, coils, width))
+    loads["kspace", p].wait()
     data = jnp.concatenate(
         [
             jnp.concatenate([kspace_ref[c, p, 0, k].astype(jnp.float32) for c in range(coils)], axis=1)
@@ -280,9 +290,10 @@
 
 def step_kernel(
     planes, frames, group, coils, width_y, width_z,
-    shifts_ref, step_ref, level_ref, offsets_ref, image_ref, sens_ref, kspace_ref, table_ref,
-    out_ref,
-    rolled, gathered, entries, inverse, finished, landed,
+    shifts_ref, step_ref, level_ref, offsets_ref, image_hbm, sens_hbm, kspace_hbm, table_hbm,
+    landed,
+    image_ref, sens_ref, kspace_ref, table_ref, load_sem,
+    rolled, gathered, entries, inverse, finished,
     send_out, recv_out, send_back, recv_back, own_out, own_back,
 ):
     total = frames * group
@@ -293,12 +304,34 @@
     me = frame_me * group + part_me
     rows = PATCH_Y
 
+    def flip(index, mask, count):
+        bit = 1
+        while bit < count:
+            if mask & bit:
+                index = index + bit - 2 * bit * lax.rem(index // bit, 2)
+            bit *= 2
+        return index
+
     def device(index):
         return {"plane": base + lax.rem(index, group), "frame": index // group}
 
+    loads = {}
+
+    def load(name, source, target):
+        loads[name] = pltpu.make_async_copy(source, target, load_sem.at[len(loads)])
+        loads[name].start()
+
+    for p in range(planes):
+        load(("image", p), image_hbm.at[p], image_ref.at[p])
+        load(("sens", p), sens_hbm.at[:, p], sens_ref.at[:, p])
+        if p == 0:
+            load("inverse", table_hbm.at[2:4], table_ref.at[2:4])
+            load("forward", table_hbm.at[0:2], table_ref.at[0:2])
+        load(("kspace", p), kspace_hbm.at[:, p], kspace_ref.at[:, p])
+
     barrier = pltpu.get_barrier_semaphore()
     for k in range(1, total):
-        pl.semaphore_signal(barrier, inc=1, device_id=device(lax.rem(me + k, total)), device_id_type=pl.DeviceIdType.MESH)
+        pl.semaphore_signal(barrier, inc=1, device_id=device(flip(me, k, total)), device_id_type=pl.DeviceIdType.MESH)
 
     lane = lax.broadcasted_iota(jnp.int32, (width_y, width_z), 1)
     row = lax.broadcasted_iota(jnp.int32, (width_y, width_z), 0)
@@ -311,14 +344,14 @@
 
     sends = []
     for p in range(planes):
-        moved = moved_plane(p, coils, width_y, image_ref, sens_ref, kspace_ref, table_ref, step_ref[0], sampled)
+        moved = moved_plane(loads, p, coils, width_y, image_ref, sens_ref, kspace_ref, table_ref, step_ref[0], sampled)
         for k in range(2):
             rolled[p, k] = pltpu.roll(pltpu.roll(moved[k], shifts_ref[0], 0), shifts_ref[1], 1)
         if p == 0:
             pl.semaphore_wait(barrier, total - 1)
         group_sends = []
-        for k in range(1, total):
-            target = lax.rem(me + k, total)
+        for k in reversed(range(1, total)):
+            target = flip(me, k, total)
             copy = pltpu.make_async_remote_copy(
                 src_ref=rolled.at[p, :, pl.ds(pl.multiple_of(target * rows, rows), rows), :],
                 dst_ref=gathered.at[p, part_me, frame_me],
@@ -380,70 +413,64 @@
             matrix[f, g] = (entries[f * frames + g], entries[g * frames + f])
     matrix = sweep(matrix, frames)
     for f, g in pairs:
-        inverse[f * frames + g] = matrix[f, g][0] * level
+        re, im = matrix[f, g]
+        inverse[f, g, 0] = re * level
         if f != g:
-            inverse[g * frames + f] = matrix[f, g][1] * level
+            inverse[f, g, 1] = im * level
+            inverse[g, f, 0] = re * level
+            inverse[g, f, 1] = -im * level
+        else:
+            inverse[f, f, 1] = jnp.zeros_like(re)
 
     backs = []
-    for r in range(group):
-        q = lax.rem(part_me + 1 + r, group)
-        for p in range(planes):
-            values = [(gathered[p, q, g, 0], gathered[p, q, g, 1]) for g in range(frames)]
-            for f in range(frames):
-                re, im = values[f]
+    spot = pl.ds(pl.multiple_of(me * rows, rows), rows)
+    for k in reversed(range(frames)):
+        f = flip(frame_me, k, frames)
+        weights = [(inverse[f, g, 0], inverse[f, g, 1]) for g in range(frames)]
+        for r in reversed(range(group)):
+            q = flip(part_me, r, group)
+            for p in range(planes):
+                re = gathered[p, q, f, 0]
+                im = gathered[p, q, f, 1]
                 for g in range(frames):
-                    g_re, g_im = values[g]
-                    if f == g:
-                        w_re = inverse[f * frames + f]
-                        re = re + w_re * g_re
-                        im = im + w_re * g_im
-                        continue
-                    if f > g:
-                        w_re, w_im = inverse[f * frames + g], inverse[g * frames + f]
-                        re = re + (w_re * g_re - w_im * g_im)
-                        im = im + (w_re * g_im + w_im * g_re)
-                    else:
-                        w_re, w_im = inverse[g * frames + f], inverse[f * frames + g]
-                        re = re + (w_re * g_re + w_im * g_im)
-                        im = im + (w_re * g_im - w_im * g_re)
+                    g_re, g_im = gathered[p, q, g, 0], gathered[p, q, g, 1]
+                    w_re, w_im = weights[g]
+                    re = re + (w_re * g_re - w_im * g_im)
+                    im = im + (w_re * g_im + w_im * g_re)
                 finished[q, f, p, 0] = re
                 finished[q, f, p, 1] = im
-        for k in range(frames):
-            f = lax.rem(frame_me + k, frames)
-            source = finished.at[q, f]
-            if r == group - 1 and k == 0:
-                copy = pltpu.make_async_copy(
-                    source, landed.at[:, :, pl.ds(pl.multiple_of(me * rows, rows), rows), :], own_back
+            if k == 0 and r == 0:
+                copy = pltpu.make_async_copy(finished.at[q, f], landed.at[:, 0, :, spot, :], own_back)
+            else:
+                copy = pltpu.make_async_remote_copy(
+                    src_ref=finished.at[q, f],
+                    dst_ref=landed.at[:, 0, :, spot, :],
+                    send_sem=send_back.at[r, k],
+                    recv_sem=recv_back.at[r, k],
+                    device_id={"plane": base + q, "frame": f},
+                    device_id_type=pl.DeviceIdType.MESH,
                 )
-                copy.start()
-                backs.append((copy, True))
-                continue
-            copy = pltpu.make_async_remote_copy(
-                src_ref=source,
-                dst_ref=landed.at[:, :, pl.ds(pl.multiple_of(me * rows, rows), rows), :],
-                send_sem=send_back.at[r, k],
-                recv_sem=recv_back.at[r, k],
-                device_id={"plane": base + q, "frame": f},
-                device_id_type=pl.DeviceIdType.MESH,
-            )
             copy.start()
-            backs.append((copy, False))
+            backs.append((copy, k == 0 and r == 0))
     for copy, local in backs:
         if local:
             copy.wait()
         else:
             copy.wait_recv()
-    for p in range(planes):
-        for k in range(2):
-            shift_y = lax.rem(width_y - shifts_ref[0], width_y)
-            shift_z = lax.rem(width_z - shifts_ref[1], width_z)
-            out_ref[p, 0, k] = pltpu.roll(pltpu.roll(landed[p, k], shift_y, 0), shift_z, 1)
     for group_sends, own in sends:
         for copy in group_sends:
             copy.wait_send()
     for copy, local in backs:
         if not local:
             copy.wait_send()
+
+
+def unroll_kernel(planes, width_y, width_z, shifts_ref, landed_ref, out_ref):
+    shift_y = lax.rem(width_y - shifts_ref[0], width_y)
+    shift_z = lax.rem(width_z - shifts_ref[1], width_z)
+    for p in range(planes):
+        for k in range(2):
+            out_ref[p, 0, k] = pltpu.roll(pltpu.roll(landed_ref[p, 0, k], shift_y, 0), shift_z, 1)
 
 
 def local_fused(image, sens, kspace, offsets, shifts, step_size, threshold):
@@ -455,20 +482,26 @@
     table = jnp.asarray(block_tables(width_y))
     vmem = pl.BlockSpec(memory_space=pltpu.VMEM)
     smem = pl.BlockSpec(memory_space=pltpu.SMEM)
+    hbm = pl.BlockSpec(memory_space=pltpu.HBM)
     slab = (PATCH_Y, width_z)
     dma = pltpu.SemaphoreType.DMA
-    return pl.pallas_call(
+    image, sens, kspace, table = [pltpu.with_memory_space_constraint(x, pltpu.HBM) for x in (image, sens, kspace, table)]
+    landed = pl.pallas_call(
         functools.partial(step_kernel, planes, frames, group, coils, width_y, width_z),
         out_shape=jax.ShapeDtypeStruct(image.shape, jnp.float32),
-        in_specs=[smem, smem, smem, vmem, vmem, vmem, vmem, vmem],
-        out_specs=vmem,
+        in_specs=[smem, smem, smem, vmem, hbm, hbm, hbm, hbm],
+        out_specs=pl.BlockSpec(memory_space=pl.ANY),
         scratch_shapes=[
+            pltpu.VMEM(image.shape, image.dtype),
+            pltpu.VMEM(sens.shape, sens.dtype),
+            pltpu.VMEM(kspace.shape, kspace.dtype),
+            pltpu.VMEM(table.shape, table.dtype),
+            dma((3 * planes + 2,)),
             pltpu.VMEM((planes, 2, width_y, width_z), jnp.float32),
             pltpu.VMEM((planes, group, frames, 2) + slab, jnp.float32),
             pltpu.VMEM((frames * frames,) + slab, jnp.float32),
-            pltpu.VMEM((frames * frames,) + slab, jnp.float32),
+            pltpu.VMEM((frames, frames, 2) + slab, jnp.float32),
             pltpu.VMEM((group, frames, planes, 2) + slab, jnp.float32),
-            pltpu.VMEM((planes, 2, width_y, width_z), jnp.float32),
             dma((planes, total)),
             dma((planes, total)),
             dma((group, frames)),
@@ -476,17 +509,25 @@
             dma((planes,)),
             dma(()),
         ],
-        compiler_params=pltpu.CompilerParams(collective_id=0, has_side_effects=True),
+        compiler_params=pltpu.CompilerParams(collective_id=0, has_side_effects=True, vmem_limit_bytes=VMEM_BYTES),
         name="prox_step",
     )(shifts, step_size, threshold, offsets, image, sens, kspace, table)
+    return pl.pallas_call(
+        functools.partial(unroll_kernel, planes, width_y, width_z),
+        out_shape=jax.ShapeDtypeStruct(image.shape, jnp.float32),
+        in_specs=[smem, vmem],
+        out_specs=vmem,
+        compiler_params=pltpu.CompilerParams(vmem_limit_bytes=VMEM_BYTES),
+        name="shift_back",
+    )(shifts, landed)
 
 
 def local(image, sens, kspace, offsets, shifts, step_size, threshold):
     planes, frames_dev, _, width_y, width_z = image.shape
     frames = frames_dev * lax.axis_size("frame")
     group = PATCH_X // planes
-    one_block = frames * group * PATCH_Y == width_y and frames_dev == 1
-    split = group > 1 and lax.axis_size("plane") % group == 0
+    one_block = frames * group * PATCH_Y == width_y and frames_dev == 1 and frames & (frames - 1) == 0
+    split = group > 1 and group & (group - 1) == 0 and lax.axis_size("plane") % group == 0
     if one_block and split and width_y == width_z and width_z % 128 == 0:
         return local_fused(image, sens, kspace, offsets, shifts, step_size, threshold)
     return local_general(image, sens, kspace, offsets, shifts, step_size, threshold)

time: 27.6 us -> 26 us (0.942)
  local copies, waits for them, and re-layouts: 1.67 us -> 0.01 us
    unnamed x1 -> x4, local copies, waits for them, and re-layouts: 1.67 us -> 0.01 us
    pallas_call x0 -> x1, Pallas kernels: none -> 1.39 us  [local_fused(): pl.pallas_call(functools.partial(unroll_kernel, planes, width_y, width_z)...]
    pallas_call x1, Pallas kernels: 24.4 us -> 23.1 us  [local_fused(): pl.pallas_call(functools.partial(step_kernel, planes, frames, group, coil...]
where the time goes in v2:
time: 26 us; the launch traced here: 25.9 us
  Pallas kernels  24.5 us (94%)
  between operations  1.36 us (5%)
    pallas_call x1, Pallas kernels, local_fused(): pl.pallas_call(functools.partial(step_kernel, planes, frames, group, coil...  23.1 us
    pallas_call x1, Pallas kernels, local_fused(): pl.pallas_call(functools.partial(unroll_kernel, planes, width_y, width_z)...  1.39 us

profile of v2, /device:TPU:0, one launch (start us, length us, event | category | flops | bytes accessed | tf_op | source)
XLA Modules:
  0.0 25.9 jit_solution(9573803834137748796)
XLA Ops:
  0.7 0.0 copy-start
  0.7 0.0 copy-start.1
  1.3 0.0 copy-done
  1.3 0.0 copy-done.1
  1.4 23.1 %prox_step.1.landed_ref = f32[2,1,2,128,128]{4,3,2,1,0:T(8,128)S(1)} custom-call(s32[2]{0:T(128)S(1)} %copy-done, f32[1]{0:T(128)S(6)} %copy.9.step_ref, f32[1]{0:T(128)S(6)} %copy.10.level_ref, s32[1,128]{1,0:T(1,128)S(1)} %copy-done.1, f32[2,1,2,128,128]{4,3,2,1,0:T(8,128)} %image_hbm.1, bf16[4,2,2,128,128]{4,3,2,1,0:T(8,128)(2,1)} %sens_hbm.1, ...), custom_call_target="tpu_custom_call" | custom-call | tf_op jit(solution)/shard_map/prox_step/pallas_call | solution.py:489
  24.5 1.4 %shift_back.1 = f32[2,1,2,128,128]{4,3,2,1,0:T(8,128)} custom-call(s32[2]{0:T(128)S(1)} %copy-done, f32[2,1,2,128,128]{4,3,2,1,0:T(8,128)S(1)} %prox_step.1.landed_ref), custom_call_target="tpu_custom_call" | custom-call | tf_op jit(solution)/shard_map/shift_back/pallas_call | solution.py:515
Async XLA Ops:
  0.7 0.7 %copy-start = (s32[2]{0:T(128)S(1)}, s32[2]{0:T(128)}, u32[]{:S(2)}) copy-start(s32[2]{0:T(128)} %shifts_ref.3) | copy-start | bytes 28
  0.7 0.7 %copy-start.1 = (s32[1,128]{1,0:T(1,128)S(1)}, s32[1,128]{1,0:T(1,128)}, u32[]{:S(2)}) copy-start(s32[1,128]{1,0:T(1,128)} %offsets_ref.1) | copy-start | bytes 1540

commit v3 on v2

--- a/solution.py
+++ b/solution.py
@@ -173,10 +173,22 @@
     angles = (indices[:, None] * indices[None, :] % length) * (2.0 * np.pi / length)
     cos = np.cos(angles) / np.sqrt(length)
     sin = np.sin(angles) / np.sqrt(length)
-    rotation = np.block([[cos, sin], [-sin, cos]])
-    high = rotation.astype(jnp.bfloat16)
-    low = (rotation - high.astype(np.float64)).astype(jnp.bfloat16)
-    return np.stack([high, low, high.T, low.T])
+    parts = []
+    for table in (cos, sin):
+        high = table.astype(jnp.bfloat16)
+        parts += [high, (table - high.astype(np.float64)).astype(jnp.bfloat16)]
+    return np.stack(parts)
+
+
+def lay_tables(parts_ref, table_ref, width):
+    low, top = pl.ds(0, width), pl.ds(width, width)
+    for k in range(2):
+        cos, sin = parts_ref[k], parts_ref[2 + k]
+        for table, upper, lower in ((k, sin, -sin), (2 + k, -sin, sin)):
+            table_ref[table, low, low] = cos
+            table_ref[table, top, top] = cos
+            table_ref[table, low, top] = upper
+            table_ref[table, top, low] = lower
 
 
 def halves(values):
@@ -214,7 +226,7 @@
     return jnp.concatenate(parts, axis=0)
 
 
-def moved_plane(loads, p, coils, width, image_ref, sens_ref, kspace_ref, table_ref, step, sampled):
+def moved_plane(loads, start_later, p, coils, width, image_ref, sens_ref, kspace_ref, table_ref, step, sampled):
     loads["image", p].wait()
     loads["sens", p].wait()
     image_re = image_ref[p, 0, 0]
@@ -228,13 +240,11 @@
                 [sens_re * image_re - sens_im * image_im, sens_re * image_im + sens_im * image_re], axis=1
             )
         )
-    if p == 0:
-        loads["inverse"].wait()
     along = from_right(jnp.concatenate(stacked, axis=0), table_ref[2], table_ref[3])
-    if p == 0:
-        loads["forward"].wait()
     spectra = from_left(table_ref[0], table_ref[1], rows_to_lanes(along, coils, width))
     loads["kspace", p].wait()
+    if p == 0:
+        start_later()
     data = jnp.concatenate(
         [
             jnp.concatenate([kspace_ref[c, p, 0, k].astype(jnp.float32) for c in range(coils)], axis=1)
@@ -292,8 +302,8 @@
     planes, frames, group, coils, width_y, width_z,
     shifts_ref, step_ref, level_ref, offsets_ref, image_hbm, sens_hbm, kspace_hbm, table_hbm,
     landed,
-    image_ref, sens_ref, kspace_ref, table_ref, load_sem,
-    rolled, gathered, entries, inverse, finished,
+    image_ref, sens_ref, kspace_ref, parts_ref, table_ref, load_sem,
+    wrapped, rolled, gathered, entries, inverse, finished,
     send_out, recv_out, send_back, recv_back, own_out, own_back,
 ):
     total = frames * group
@@ -321,13 +331,17 @@
         loads[name] = pltpu.make_async_copy(source, target, load_sem.at[len(loads)])
         loads[name].start()
 
-    for p in range(planes):
+    def load_plane(p):
         load(("image", p), image_hbm.at[p], image_ref.at[p])
         load(("sens", p), sens_hbm.at[:, p], sens_ref.at[:, p])
-        if p == 0:
-            load("inverse", table_hbm.at[2:4], table_ref.at[2:4])
-            load("forward", table_hbm.at[0:2], table_ref.at[0:2])
         load(("kspace", p), kspace_hbm.at[:, p], kspace_ref.at[:, p])
+
+    def start_later():
+        for p in range(1, planes):
+            load_plane(p)
+
+    load("table", table_hbm, parts_ref)
+    load_plane(0)
 
     barrier = pltpu.get_barrier_semaphore()
     for k in range(1, total):
@@ -343,10 +357,15 @@
     sampled = (regular | (low_y & low_z)).astype(jnp.float32)
 
     sends = []
+    loads["table"].wait()
+    lay_tables(parts_ref, table_ref, width_y)
     for p in range(planes):
-        moved = moved_plane(loads, p, coils, width_y, image_ref, sens_ref, kspace_ref, table_ref, step_ref[0], sampled)
+        moved = moved_plane(loads, start_later, p, coils, width_y, image_ref, sens_ref, kspace_ref, table_ref, step_ref[0], sampled)
         for k in range(2):
-            rolled[p, k] = pltpu.roll(pltpu.roll(moved[k], shifts_ref[0], 0), shifts_ref[1], 1)
+            part = pltpu.roll(moved[k], shifts_ref[1], 1)
+            wrapped[p, k, pl.ds(0, rows), :] = part[width_y - rows :]
+            wrapped[p, k, pl.ds(rows, width_y), :] = part
+            rolled[p, k] = wrapped[p, k, pl.ds(rows - shifts_ref[0], width_y), :]
         if p == 0:
             pl.semaphore_wait(barrier, total - 1)
         group_sends = []
@@ -465,12 +484,14 @@
             copy.wait_send()
 
 
-def unroll_kernel(planes, width_y, width_z, shifts_ref, landed_ref, out_ref):
-    shift_y = lax.rem(width_y - shifts_ref[0], width_y)
+def unroll_kernel(planes, width_y, width_z, shifts_ref, landed_ref, out_ref, wrapped):
     shift_z = lax.rem(width_z - shifts_ref[1], width_z)
     for p in range(planes):
         for k in range(2):
-            out_ref[p, 0, k] = pltpu.roll(pltpu.roll(landed_ref[p, 0, k], shift_y, 0), shift_z, 1)
+            part = pltpu.roll(landed_ref[p, 0, k], shift_z, 1)
+            wrapped[p, k, pl.ds(0, width_y), :] = part
+            wrapped[p, k, pl.ds(width_y, PATCH_Y), :] = part[:PATCH_Y]
+            out_ref[p, 0, k] = wrapped[p, k, pl.ds(shifts_ref[0], width_y), :]
 
 
 def local_fused(image, sens, kspace, offsets, shifts, step_size, threshold):
@@ -496,7 +517,9 @@
             pltpu.VMEM(sens.shape, sens.dtype),
             pltpu.VMEM(kspace.shape, kspace.dtype),
             pltpu.VMEM(table.shape, table.dtype),
-            dma((3 * planes + 2,)),
+            pltpu.VMEM((4, 2 * width_y, 2 * width_y), table.dtype),
+            dma((3 * planes + 1,)),
+            pltpu.VMEM((planes, 2, width_y + PATCH_Y, width_z), jnp.float32),
             pltpu.VMEM((planes, 2, width_y, width_z), jnp.float32),
             pltpu.VMEM((planes, group, frames, 2) + slab, jnp.float32),
             pltpu.VMEM((frames * frames,) + slab, jnp.float32),
@@ -517,6 +540,7 @@
         out_shape=jax.ShapeDtypeStruct(image.shape, jnp.float32),
         in_specs=[smem, vmem],
         out_specs=vmem,
+        scratch_shapes=[pltpu.VMEM((planes, 2, width_y + PATCH_Y, width_z), jnp.float32)],
         compiler_params=pltpu.CompilerParams(vmem_limit_bytes=VMEM_BYTES),
         name="shift_back",
     )(shifts, landed)

time: 26 us -> 26 us (level)
  no operation moved by 1% of the time
where the time goes in v3:
time: 26 us; the launch traced here: 25.9 us
  Pallas kernels  24.5 us (94%)
  between operations  1.36 us (5%)
    pallas_call x1, Pallas kernels, local_fused(): pl.pallas_call(functools.partial(step_kernel, planes, frames, group, coil...  23.1 us
    pallas_call x1, Pallas kernels, local_fused(): pl.pallas_call(functools.partial(unroll_kernel, planes, width_y, width_z)...  1.39 us

profile of v3, /device:TPU:0, one launch (start us, length us, event | category | flops | bytes accessed | tf_op | source)
XLA Modules:
  0.0 25.9 jit_solution(6485170639790242673)
XLA Ops:
  0.7 0.0 copy-start
  0.7 0.0 copy-start.1
  1.3 0.0 copy-done
  1.3 0.0 copy-done.1
  1.4 23.1 %prox_step.1.landed_ref = f32[2,1,2,128,128]{4,3,2,1,0:T(8,128)S(1)} custom-call(s32[2]{0:T(128)S(1)} %copy-done, f32[1]{0:T(128)S(6)} %copy.9.step_ref, f32[1]{0:T(128)S(6)} %copy.10.level_ref, s32[1,128]{1,0:T(1,128)S(1)} %copy-done.1, f32[2,1,2,128,128]{4,3,2,1,0:T(8,128)} %image_hbm.1, bf16[4,2,2,128,128]{4,3,2,1,0:T(8,128)(2,1)} %sens_hbm.1, ...), custom_call_target="tpu_custom_call" | custom-call | tf_op jit(solution)/shard_map/prox_step/pallas_call | solution.py:510
  24.5 1.4 %shift_back.1 = f32[2,1,2,128,128]{4,3,2,1,0:T(8,128)} custom-call(s32[2]{0:T(128)S(1)} %copy-done, f32[2,1,2,128,128]{4,3,2,1,0:T(8,128)S(1)} %prox_step.1.landed_ref), custom_call_target="tpu_custom_call" | custom-call | tf_op jit(solution)/shard_map/shift_back/pallas_call | solution.py:538
Async XLA Ops:
  0.7 0.7 %copy-start = (s32[2]{0:T(128)S(1)}, s32[2]{0:T(128)}, u32[]{:S(2)}) copy-start(s32[2]{0:T(128)} %shifts_ref.3) | copy-start | bytes 28
  0.7 0.7 %copy-start.1 = (s32[1,128]{1,0:T(1,128)S(1)}, s32[1,128]{1,0:T(1,128)}, u32[]{:S(2)}) copy-start(s32[1,128]{1,0:T(1,128)} %offsets_ref.1) | copy-start | bytes 1540
